TPU v7x, 32 devices: a whole 2x2x4 slice. The times are simulated.
32 devices in a mesh: dp: 8 (over z, y), mp: 4 (over x, core).
Axes of the slice: x: 2, y: 2, z: 4, core: 2. Of those that a mesh axis runs over, the one named last changes fastest.
Arguments:
- acts: bfloat16 [8192, 2048], P('dp', 'mp'), may hold values from -6 to 6
- out_grads: bfloat16 [2, 28672, 2048], P(None, 'dp', 'mp'), may hold values from -0.125 to 0.125
- proj_old: float32 [2, 8192, 256], P(None, 'dp'), may hold values from -0.0625 to 0.0625
- moment_one: float32 [2, 28672, 256], P(None, 'dp', 'mp'), may hold values from -12 to 12
- moment_two: float32 [2, 28672, 256], P(None, 'dp', 'mp'), may hold values from 1 to 20
Outputs:
- proj_new: float32 [2, 8192, 256], P(None, 'dp')
- first_new: float32 [2, 28672, 256], P(None, 'dp', 'mp')
- second_new: float32 [2, 28672, 256], P(None, 'dp', 'mp')
- step_update: float32 [2, 28672, 256], P(None, 'dp', 'mp')
All inputs are finite; a program needn't handle non-finite values.
Results may differ from a plain program's by a relative error of at most 0.03.
Values may be sent and summed in bfloat16 or wider, within the bound.
A program may use at most 128 MiB of HBM per device.

v0:
```python
import jax
import jax.numpy as jnp
from jax import lax
from jax.sharding import PartitionSpec as P

SWEEPS = 2


def orthonormal(image, gram):
    lower = jnp.linalg.cholesky(gram)
    solved = jax.scipy.linalg.solve_triangular(lower, jnp.swapaxes(image, 1, 2), lower=True)
    return jnp.swapaxes(solved, 1, 2)


def shards(acts, out_grads, proj_old, moment_one, moment_two):

    def grads_fold(piece):
        return jnp.einsum("kft,tkr->kfr", out_grads, piece, preferred_element_type=jnp.float32)

    def token_product(basis):
        basis_half = basis.astype(jnp.bfloat16)
        local = jnp.einsum("dt,kdr->tkr", acts, basis_half, preferred_element_type=jnp.float32)
        share = lax.psum_scatter(local, "dp", scatter_dimension=0, tiled=True).astype(jnp.bfloat16)
        coeff = lax.all_gather(share, "dp", axis=0, tiled=True)
        return grads_fold(coeff)

    basis = proj_old
    for sweep in range(SWEEPS):
        hidden_part = token_product(basis)
        hidden_share = lax.psum_scatter(
            hidden_part.astype(jnp.bfloat16), "mp", scatter_dimension=1, tiled=True
        )
        token_part = jnp.einsum(
            "kft,kfr->tkr",
            out_grads,
            lax.all_gather(hidden_share, "mp", axis=1, tiled=True),
            preferred_element_type=jnp.float32,
        )
        token_share = lax.psum_scatter(token_part, "dp", scatter_dimension=0, tiled=True).astype(
            jnp.bfloat16
        )
        image_part = jnp.einsum(
            "dt,tkr->kdr",
            acts,
            lax.all_gather(token_share, "dp", axis=0, tiled=True),
            preferred_element_type=jnp.float32,
        )
        image = lax.psum(image_part.astype(jnp.bfloat16), "mp").astype(jnp.float32)
        gram_local = jnp.einsum("kdr,kds->krs", image, image, precision=lax.Precision.HIGHEST)
        gram = lax.psum(gram_local, "dp")
        basis = orthonormal(image, gram)
    projected_part = token_product(basis)
    projected = lax.psum_scatter(
        projected_part.astype(jnp.bfloat16), "mp", scatter_dimension=2, tiled=True
    ).astype(jnp.float32)
    first_new = 0.9 * moment_one + 0.1 * projected
    second_new = 0.999 * moment_two + 0.001 * projected * projected
    step_update = first_new / (jnp.sqrt(second_new) + 1e-08)
    return (basis, first_new, second_new, step_update)


def solution(mesh):
    placed = (
        P("dp", "mp"),
        P(None, "dp", "mp"),
        P(None, "dp", None),
        P(None, "dp", "mp"),
        P(None, "dp", "mp"),
    )
    return jax.shard_map(
        shards,
        mesh=mesh,
        in_specs=placed,
        out_specs=(
            P(None, "dp", None),
            P(None, "dp", "mp"),
            P(None, "dp", "mp"),
            P(None, "dp", "mp"),
        ),
        check_vma=False,
    )
```

profile of v0, /device:TPU:0, one launch (start us, length us, event | category | flops | bytes accessed | tf_op | source)
XLA Modules:
  0.0 1283.0 jit_solution(4463060384800956341)
XLA Ops:
  11.5 74.2 %all-reduce.23 = bf16[512,2,256]{2,1,0:T(2,128)(2,1)S(1)} all-reduce(f32[512,2,256]{2,1,0:T(2,128)S(1)} %copy.67), channel_id=2, replica_groups=mesh['dp'=8,'mp'=4] {'dp'}, use_global_device_ids=true, to_apply=%region_0.0.clone | all-reduce | flops 262144 | bytes 1572864
  87.1 31.5 %all_gather.21 = bf16[512,2,256]{2,1,0:T(2,128)(2,1)S(1)} all-gather(bf16[64,2,256]{2,1,0:T(2,128)(2,1)S(1)} %dynamic-slice_convert_fusion.4), channel_id=1, replica_groups=mesh['dp'=8,'mp'=4] {'dp'}, dimensions={0}, use_global_device_ids=true | all-gather | bytes 589824 | tf_op jit(solution)/shard_map/all_gather | solution.py:24
  140.1 40.0 %reduce-scatter.10.cloned.1.call-done = bf16[896,512]{1,0:T(8,128)(2,1)} async-done(((bf16[3584,512]{1,0:T(8,128)(2,1)}), bf16[896,512]{1,0:T(8,128)(2,1)}) %reduce-scatter.10.cloned.1.call-update) | async-done | bytes 917520
  185.2 31.6 %all-gather.3.cloned.1.call-done = bf16[2,3584,256]{1,2,0:T(8,128)(2,1)} async-done(((bf16[2,896,256]{1,2,0:T(8,128)(2,1)}), bf16[2,3584,256]{1,2,0:T(8,128)(2,1)}) %all-gather.3.cloned.1.call-update) | async-done | bytes 3670032 | tf_op jit(solution)/shard_map/all_gather | solution.py:36
  223.6 72.5 %all-reduce.24 = bf16[512,2,256]{2,1,0:T(2,128)(2,1)S(1)} all-reduce(f32[512,2,256]{2,1,0:T(2,128)S(1)} %copy.69), channel_id=4, replica_groups=mesh['dp'=8,'mp'=4] {'dp'}, use_global_device_ids=true, to_apply=%region_2.0.clone | all-reduce | flops 262144 | bytes 1572864
  296.2 31.4 %all_gather.23 = bf16[512,2,256]{2,1,0:T(2,128)(2,1)S(1)} all-gather(bf16[64,2,256]{2,1,0:T(2,128)(2,1)S(1)} %dynamic-slice_convert_fusion.3), channel_id=1, replica_groups=mesh['dp'=8,'mp'=4] {'dp'}, dimensions={0}, use_global_device_ids=true | all-gather | bytes 589824 | tf_op jit(solution)/shard_map/all_gather | solution.py:45
  329.4 33.4 %all-reduce.16.cloned.1.call-done = bf16[2,1024,256]{1,2,0:T(8,128)(2,1)} async-done(((bf16[2,1024,256]{1,2,0:T(8,128)(2,1)}), bf16[2,1024,256]{1,2,0:T(8,128)(2,1)}) %all-reduce.16.cloned.1.call-update) | async-done | bytes 1048592 | tf_op jit(solution)/shard_map/psum | solution.py:48
  367.6 71.9 %all-reduce.18.cloned.1.call-done = f32[2,256,256]{1,2,0:T(8,128)} async-done(((f32[2,256,256]{1,2,0:T(8,128)}), f32[2,256,256]{1,2,0:T(8,128)}) %all-reduce.18.cloned.1.call-update) | async-done | bytes 524304 | tf_op jit(solution)/shard_map/psum | solution.py:50
  442.7 23.5 %custom-call.17 = f32[2,128,128]{2,1,0:T(8,128)S(1)} custom-call(f32[2,128,128]{2,1,0:T(8,128)S(1)} %cholesky.198), custom_call_target="Cholesky" | custom-call | tf_op jit(solution)/shard_map/jit(cholesky)/cholesky | solution.py:10
  490.6 24.3 %custom-call.19 = f32[2,128,128]{2,1,0:T(8,128)S(1)} custom-call(f32[2,128,128]{2,1,0:T(8,128)} %convolution_subtract_fusion.3), custom_call_target="Cholesky" | custom-call | tf_op jit(solution)/shard_map/jit(cholesky)/cholesky | solution.py:10
  525.8 41.1 %custom-call.20 = f32[2,2,128,128]{2,3,1,0:T(8,128)} custom-call(f32[2,2,128,128]{3,2,1,0:T(8,128)} %bitcast.143), custom_call_target="InvertDiagBlocksLowerTriangular" | custom-call | tf_op jit(solution)/shard_map/jit(_solve_triangular)/vmap()/triangular_solve | solution.py:11
  573.2 71.6 %all-reduce.25 = bf16[512,2,256]{2,1,0:T(2,128)(2,1)S(1)} all-reduce(f32[512,2,256]{2,1,0:T(2,128)S(1)} %copy.79), channel_id=5, replica_groups=mesh['dp'=8,'mp'=4] {'dp'}, use_global_device_ids=true, to_apply=%region_9.0.clone | all-reduce | flops 262144 | bytes 1572864
  644.9 31.5 %all_gather.24 = bf16[512,2,256]{2,1,0:T(2,128)(2,1)S(1)} all-gather(bf16[64,2,256]{2,1,0:T(2,128)(2,1)S(1)} %dynamic-slice_convert_fusion.2), channel_id=1, replica_groups=mesh['dp'=8,'mp'=4] {'dp'}, dimensions={0}, use_global_device_ids=true | all-gather | bytes 589824 | tf_op jit(solution)/shard_map/all_gather | solution.py:24
  698.0 39.0 %reduce-scatter.12.cloned.1.call-done = bf16[896,512]{1,0:T(8,128)(2,1)} async-done(((bf16[3584,512]{1,0:T(8,128)(2,1)}), bf16[896,512]{1,0:T(8,128)(2,1)}) %reduce-scatter.12.cloned.1.call-update) | async-done | bytes 917520
  742.1 31.4 %all-gather.5.cloned.1.call-done = bf16[2,3584,256]{1,2,0:T(8,128)(2,1)} async-done(((bf16[2,896,256]{1,2,0:T(8,128)(2,1)}), bf16[2,3584,256]{1,2,0:T(8,128)(2,1)}) %all-gather.5.cloned.1.call-update) | async-done | bytes 3670032 | tf_op jit(solution)/shard_map/all_gather | solution.py:36
  780.4 72.5 %all-reduce.26 = bf16[512,2,256]{2,1,0:T(2,128)(2,1)S(1)} all-reduce(f32[512,2,256]{2,1,0:T(2,128)S(1)} %copy.81), channel_id=7, replica_groups=mesh['dp'=8,'mp'=4] {'dp'}, use_global_device_ids=true, to_apply=%region_11.0.clone | all-reduce | flops 262144 | bytes 1572864
  853.0 31.4 %all_gather.26 = bf16[512,2,256]{2,1,0:T(2,128)(2,1)S(1)} all-gather(bf16[64,2,256]{2,1,0:T(2,128)(2,1)S(1)} %dynamic-slice_convert_fusion.1), channel_id=1, replica_groups=mesh['dp'=8,'mp'=4] {'dp'}, dimensions={0}, use_global_device_ids=true | all-gather | bytes 589824 | tf_op jit(solution)/shard_map/all_gather | solution.py:45
  886.2 33.5 %all-reduce.20.cloned.1.call-done = bf16[2,1024,256]{1,2,0:T(8,128)(2,1)} async-done(((bf16[2,1024,256]{1,2,0:T(8,128)(2,1)}), bf16[2,1024,256]{1,2,0:T(8,128)(2,1)}) %all-reduce.20.cloned.1.call-update) | async-done | bytes 1048592 | tf_op jit(solution)/shard_map/psum | solution.py:48
  924.2 72.6 %all-reduce.22.cloned.1.call-done = f32[2,256,256]{1,2,0:T(8,128)} async-done(((f32[2,256,256]{1,2,0:T(8,128)}), f32[2,256,256]{1,2,0:T(8,128)}) %all-reduce.22.cloned.1.call-update) | async-done | bytes 524304 | tf_op jit(solution)/shard_map/psum | solution.py:50
  999.2 23.5 %custom-call.21 = f32[2,128,128]{2,1,0:T(8,128)S(1)} custom-call(f32[2,128,128]{2,1,0:T(8,128)S(1)} %cholesky.201), custom_call_target="Cholesky" | custom-call | tf_op jit(solution)/shard_map/jit(cholesky)/cholesky | solution.py:10
  1071.1 39.5 %custom-call.24 = f32[2,2,128,128]{2,3,1,0:T(8,128)S(1)} custom-call(f32[2,2,128,128]{3,2,1,0:T(8,128)S(1)} %bitcast.142), custom_call_target="InvertDiagBlocksLowerTriangular" | custom-call | tf_op jit(solution)/shard_map/jit(_solve_triangular)/vmap()/triangular_solve | solution.py:11
  1120.1 72.8 %all-reduce.27 = bf16[512,2,256]{2,1,0:T(2,128)(2,1)} all-reduce(f32[512,2,256]{2,1,0:T(2,128)} %copy.91), channel_id=8, replica_groups=mesh['dp'=8,'mp'=4] {'dp'}, use_global_device_ids=true, to_apply=%region_14.17.clone | all-reduce | flops 262144 | bytes 1572864
  1193.8 31.7 %all_gather.27 = bf16[512,2,256]{2,1,0:T(2,128)(2,1)S(1)} all-gather(bf16[64,2,256]{2,1,0:T(2,128)(2,1)S(1)} %dynamic-slice_convert_fusion), channel_id=1, replica_groups=mesh['dp'=8,'mp'=4] {'dp'}, dimensions={0}, use_global_device_ids=true | all-gather | bytes 589824 | tf_op jit(solution)/shard_map/all_gather | solution.py:24
  1237.2 34.3 %reduce-scatter.8.cloned.1.call-done = bf16[2,3584,64]{1,2,0:T(8,128)(2,1)} async-done(((bf16[2,3584,256]{1,2,0:T(8,128)(2,1)}), bf16[2,3584,64]{1,2,0:T(8,128)(2,1)}) %reduce-scatter.8.cloned.1.call-update) | async-done | bytes 917520 | tf_op jit(solution)/shard_map/reduce_scatter | solution.py:53
  (123 shorter events, 218.4 us)
Async XLA Ops:
  7.2 1.2 copy-start
  7.2 173.0 %reduce-scatter.10.cloned.1.call-start = ((), (), s32[]{:S(2)}) async-start(), calls=%async_computation.10 | async-start | bytes 4587520
  10.7 75.1 %copy-start.7 = (u32[32]{0:T(128)S(1)}, u32[32]{0:T(128)}, u32[]{:S(2)}) copy-start(u32[32]{0:T(128)} %constant.98) | copy-start | bytes 388
  140.1 76.7 %all-gather.3.cloned.1.call-start = ((), (), s32[]{:S(2)}) async-start(), calls=%async_computation.3 | async-start | bytes 4587520 | tf_op jit(solution)/shard_map/all_gather | solution.py:36
  185.1 177.7 %all-reduce.16.cloned.1.call-start = ((), (), s32[]{:S(2)}) async-start(), calls=%async_computation.4 | async-start | bytes 2097152 | tf_op jit(solution)/shard_map/psum | solution.py:48
  329.3 110.2 %all-reduce.18.cloned.1.call-start = ((), (), s32[]{:S(2)}) async-start(), calls=%async_computation.5 | async-start | bytes 1048576 | tf_op jit(solution)/shard_map/psum | solution.py:50
  362.9 3.2 copy-start.1
  365.8 371.1 %reduce-scatter.12.cloned.1.call-start = ((), (), s32[]{:S(2)}) async-start(), calls=%async_computation.11 | async-start | bytes 4587520
  441.9 0.8 copy-start.5
  486.7 80.3 %copy-start.3 = (f32[2,256,1024]{2,1,0:T(8,128)S(1)}, f32[2,256,1024]{2,1,0:T(8,128)}, u32[]{:S(2)}) copy-start(f32[2,256,1024]{2,1,0:T(8,128)} %convert_bitcast_fusion.1) | copy-start | bytes 6291460
  568.9 2.0 copy-start.6
  697.9 75.6 %all-gather.5.cloned.1.call-start = ((), (), s32[]{:S(2)}) async-start(), calls=%async_computation.6 | async-start | bytes 4587520 | tf_op jit(solution)/shard_map/all_gather | solution.py:36
  741.9 177.7 %all-reduce.20.cloned.1.call-start = ((), (), s32[]{:S(2)}) async-start(), calls=%async_computation.7 | async-start | bytes 2097152 | tf_op jit(solution)/shard_map/psum | solution.py:48
  886.1 110.7 %all-reduce.22.cloned.1.call-start = ((), (), s32[]{:S(2)}) async-start(), calls=%async_computation.8 | async-start | bytes 1048576 | tf_op jit(solution)/shard_map/psum | solution.py:50
  919.6 3.0 copy-start.2
  922.6 348.9 %reduce-scatter.8.cloned.1.call-start = ((), (), s32[]{:S(2)}) async-start(), calls=%async_computation.9 | async-start | bytes 4587520 | tf_op jit(solution)/shard_map/reduce_scatter | solution.py:53
  1234.0 37.5 %copy-start.4 = (f32[2,3584,64]{1,2,0:T(8,128)S(1)}, f32[2,3584,64]{1,2,0:T(8,128)}, u32[]{:S(2)}) copy-start(f32[2,3584,64]{1,2,0:T(8,128)} %param.12) | copy-start | bytes 5505028
Sparse Core Ops, SparseCore 0:
  140.2 39.8 reduce-scatter.9
  185.3 31.4 all-gather.2
  329.4 33.3 all-reduce.15
  366.7 72.7 all-reduce.17
  698.0 38.8 reduce-scatter.11
  742.0 31.4 all-gather.4
  886.2 33.3 all-reduce.19
  924.0 72.7 all-reduce.21
  1232.7 38.7 reduce-scatter.7
where the time goes:
time: 1290 us; the launch traced here: 1280 us
  blocking collectives  521 us (40%)
  waiting for transfers between devices  388 us (30%)
  other arithmetic  230 us (18%)
  local copies, waits for them, and re-layouts  65.7 us (5%)
  matrix products  62.8 us (5%)
  between operations  15.2 us (1%)
    unnamed x5, blocking collectives  364 us
    psum x2, waiting for transfers between devices, shards(): gram = lax.psum(gram_local, 'dp')  145 us
    another operation x17, other arithmetic, orthonormal(): lower = jnp.linalg.cholesky(gram)  135 us
    all_gather x3, blocking collectives, token_product(): coeff = lax.all_gather(share, 'dp', axis=0, tiled=True)  94.8 us
    another operation x6, other arithmetic, orthonormal(): jax.scipy.linalg.solve_triangular(lower, jnp.swapaxes(image, 1, 2), lower...  82.8 us
    unnamed x11, waiting for transfers between devices  79.1 us
    psum x2, waiting for transfers between devices, shards(): image = lax.psum(image_part.astype(jnp.bfloat16), 'mp').astype(jnp.float32)  66.9 us
    all_gather x2, waiting for transfers between devices, shards(): lax.all_gather(hidden_share, 'mp', axis=1, tiled=True)  63 us
  transfers between devices with their start and end apart: 9, of which 9 were waited for; matrix products, arithmetic and copies ran while one was open for 1% of the time, Pallas kernels for 0%

commit v1 on v0

--- a/solution.py
+++ b/solution.py
@@ -4,6 +4,15 @@
 from jax.sharding import PartitionSpec as P
 
 SWEEPS = 2
+
+
+def _reach_tails(mine_x):
+    size_here = lax.psum(1, "dp")
+    val2 = lambda passed: [(ii, ii ^ passed) for ii in range(size_here)]
+    b_next = mine_x
+    for dev_j in range(size_here.bit_length() - 1):
+        b_next = b_next + lax.ppermute(b_next, axis_name="dp", perm=val2(1 << dev_j))
+    return b_next
 
 
 def orthonormal(image, gram):
@@ -47,7 +56,7 @@
         )
         image = lax.psum(image_part.astype(jnp.bfloat16), "mp").astype(jnp.float32)
         gram_local = jnp.einsum("kdr,kds->krs", image, image, precision=lax.Precision.HIGHEST)
-        gram = lax.psum(gram_local, "dp")
+        gram = _reach_tails(gram_local)
         basis = orthonormal(image, gram)
     projected_part = token_product(basis)
     projected = lax.psum_scatter(

time: 1290 us -> 1240 us (0.961)
  waiting for transfers between devices: 388 us -> 332 us
    psum x2 -> x0, waiting for transfers between devices: 145 us -> none  [shards(): gram = lax.psum(gram_local, 'dp')]
    ppermute x0 -> x6, waiting for transfers between devices: none -> 87 us  [_reach_tails(): lax.ppermute(b_next, axis_name='dp', perm=val2(1 << dev_j))]
    unnamed x11 -> x9, waiting for transfers between devices: 79.1 us -> 79.8 us
  transfers between devices with their start and end apart: 9 -> 13, of which waited for: 9 -> 13; matrix products, arithmetic and copies ran while one was open for 1% -> 1% of each run, Pallas kernels for 0% -> 0%
where the time goes in v1:
time: 1240 us; the launch traced here: 1230 us
  blocking collectives  522 us (42%)
  waiting for transfers between devices  332 us (27%)
  other arithmetic  228 us (18%)
  local copies, waits for them, and re-layouts  63.4 us (5%)
  matrix products  61 us (5%)
  between operations  15.5 us (1%)
    unnamed x5, blocking collectives  364 us
    another operation x17, other arithmetic, orthonormal(): lower = jnp.linalg.cholesky(gram)  135 us
    all_gather x3, blocking collectives, token_product(): coeff = lax.all_gather(share, 'dp', axis=0, tiled=True)  94.6 us
    ppermute x6, waiting for transfers between devices, _reach_tails(): lax.ppermute(b_next, axis_name='dp', perm=val2(1 << dev_j))  87 us
    another operation x6, other arithmetic, orthonormal(): jax.scipy.linalg.solve_triangular(lower, jnp.swapaxes(image, 1, 2), lower...  82.8 us
    unnamed x9, waiting for transfers between devices  79.8 us
    psum x2, waiting for transfers between devices, shards(): image = lax.psum(image_part.astype(jnp.bfloat16), 'mp').astype(jnp.float32)  66.5 us
    all_gather x2, waiting for transfers between devices, shards(): lax.all_gather(hidden_share, 'mp', axis=1, tiled=True)  63.2 us
  transfers between devices with their start and end apart: 13, of which 13 were waited for; matrix products, arithmetic and copies ran while one was open for 1% of the time, Pallas kernels for 0%

profile of v1, /device:TPU:0, one launch (start us, length us, event | category | flops | bytes accessed | tf_op | source)
XLA Modules:
  0.0 1231.3 jit_solution(15317611337338715087)
XLA Ops:
  11.5 74.2 %all-reduce.17 = bf16[512,2,256]{2,1,0:T(2,128)(2,1)S(1)} all-reduce(f32[512,2,256]{2,1,0:T(2,128)S(1)} %copy.73), channel_id=2, replica_groups=mesh['dp'=8,'mp'=4] {'dp'}, use_global_device_ids=true, to_apply=%region_0.0.clone | all-reduce | flops 262144 | bytes 1572864
  87.1 31.5 %all_gather.21 = bf16[512,2,256]{2,1,0:T(2,128)(2,1)S(1)} all-gather(bf16[64,2,256]{2,1,0:T(2,128)(2,1)S(1)} %dynamic-slice_convert_fusion.4), channel_id=1, replica_groups=mesh['dp'=8,'mp'=4] {'dp'}, dimensions={0}, use_global_device_ids=true | all-gather | bytes 589824 | tf_op jit(solution)/shard_map/all_gather | solution.py:33
  140.1 40.0 %reduce-scatter.10.cloned.1.call-done = bf16[896,512]{1,0:T(8,128)(2,1)} async-done(((bf16[3584,512]{1,0:T(8,128)(2,1)}), bf16[896,512]{1,0:T(8,128)(2,1)}) %reduce-scatter.10.cloned.1.call-update) | async-done | bytes 917520
  185.2 31.6 %all-gather.3.cloned.1.call-done = bf16[2,3584,256]{1,2,0:T(8,128)(2,1)} async-done(((bf16[2,896,256]{1,2,0:T(8,128)(2,1)}), bf16[2,3584,256]{1,2,0:T(8,128)(2,1)}) %all-gather.3.cloned.1.call-update) | async-done | bytes 3670032 | tf_op jit(solution)/shard_map/all_gather | solution.py:45
  223.6 72.5 %all-reduce.18 = bf16[512,2,256]{2,1,0:T(2,128)(2,1)S(1)} all-reduce(f32[512,2,256]{2,1,0:T(2,128)S(1)} %copy.75), channel_id=4, replica_groups=mesh['dp'=8,'mp'=4] {'dp'}, use_global_device_ids=true, to_apply=%region_2.0.clone | all-reduce | flops 262144 | bytes 1572864
  296.2 31.4 %all_gather.23 = bf16[512,2,256]{2,1,0:T(2,128)(2,1)S(1)} all-gather(bf16[64,2,256]{2,1,0:T(2,128)(2,1)S(1)} %dynamic-slice_convert_fusion.3), channel_id=1, replica_groups=mesh['dp'=8,'mp'=4] {'dp'}, dimensions={0}, use_global_device_ids=true | all-gather | bytes 589824 | tf_op jit(solution)/shard_map/all_gather | solution.py:54
  329.6 33.3 %all-reduce.14.cloned.1.call-done = bf16[2,1024,256]{1,2,0:T(8,128)(2,1)} async-done(((bf16[2,1024,256]{1,2,0:T(8,128)(2,1)}), bf16[2,1024,256]{1,2,0:T(8,128)(2,1)}) %all-reduce.14.cloned.1.call-update) | async-done | bytes 1048592 | tf_op jit(solution)/shard_map/psum | solution.py:57
  416.1 23.5 %custom-call.17 = f32[2,128,128]{2,1,0:T(8,128)S(1)} custom-call(f32[2,128,128]{2,1,0:T(8,128)S(1)} %cholesky.198), custom_call_target="Cholesky" | custom-call | tf_op jit(solution)/shard_map/jit(cholesky)/cholesky | solution.py:19
  464.1 24.3 %custom-call.19 = f32[2,128,128]{2,1,0:T(8,128)S(1)} custom-call(f32[2,128,128]{2,1,0:T(8,128)} %slice_subtract_fusion.1), custom_call_target="Cholesky" | custom-call | tf_op jit(solution)/shard_map/jit(cholesky)/cholesky | solution.py:19
  499.2 41.1 %custom-call.20 = f32[2,2,128,128]{2,3,1,0:T(8,128)} custom-call(f32[2,2,128,128]{3,2,1,0:T(8,128)} %bitcast.143), custom_call_target="InvertDiagBlocksLowerTriangular" | custom-call | tf_op jit(solution)/shard_map/jit(_solve_triangular)/vmap()/triangular_solve | solution.py:20
  546.7 72.1 %all-reduce.19 = bf16[512,2,256]{2,1,0:T(2,128)(2,1)S(1)} all-reduce(f32[512,2,256]{2,1,0:T(2,128)S(1)} %copy.86), channel_id=5, replica_groups=mesh['dp'=8,'mp'=4] {'dp'}, use_global_device_ids=true, to_apply=%region_8.0.clone | all-reduce | flops 262144 | bytes 1572864
  618.9 31.3 %all_gather.24 = bf16[512,2,256]{2,1,0:T(2,128)(2,1)S(1)} all-gather(bf16[64,2,256]{2,1,0:T(2,128)(2,1)S(1)} %dynamic-slice_convert_fusion.2), channel_id=1, replica_groups=mesh['dp'=8,'mp'=4] {'dp'}, dimensions={0}, use_global_device_ids=true | all-gather | bytes 589824 | tf_op jit(solution)/shard_map/all_gather | solution.py:33
  671.7 39.7 %reduce-scatter.12.cloned.1.call-done = bf16[896,512]{1,0:T(8,128)(2,1)} async-done(((bf16[3584,512]{1,0:T(8,128)(2,1)}), bf16[896,512]{1,0:T(8,128)(2,1)}) %reduce-scatter.12.cloned.1.call-update) | async-done | bytes 917520
  716.4 31.6 %all-gather.5.cloned.1.call-done = bf16[2,3584,256]{1,2,0:T(8,128)(2,1)} async-done(((bf16[2,896,256]{1,2,0:T(8,128)(2,1)}), bf16[2,3584,256]{1,2,0:T(8,128)(2,1)}) %all-gather.5.cloned.1.call-update) | async-done | bytes 3670032 | tf_op jit(solution)/shard_map/all_gather | solution.py:45
  754.9 72.5 %all-reduce.20 = bf16[512,2,256]{2,1,0:T(2,128)(2,1)S(1)} all-reduce(f32[512,2,256]{2,1,0:T(2,128)S(1)} %copy.88), channel_id=7, replica_groups=mesh['dp'=8,'mp'=4] {'dp'}, use_global_device_ids=true, to_apply=%region_10.13.clone | all-reduce | flops 262144 | bytes 1572864
  827.4 31.4 %all_gather.26 = bf16[512,2,256]{2,1,0:T(2,128)(2,1)S(1)} all-gather(bf16[64,2,256]{2,1,0:T(2,128)(2,1)S(1)} %dynamic-slice_convert_fusion.1), channel_id=1, replica_groups=mesh['dp'=8,'mp'=4] {'dp'}, dimensions={0}, use_global_device_ids=true | all-gather | bytes 589824 | tf_op jit(solution)/shard_map/all_gather | solution.py:54
  860.8 33.2 %all-reduce.16.cloned.1.call-done = bf16[2,1024,256]{1,2,0:T(8,128)(2,1)} async-done(((bf16[2,1024,256]{1,2,0:T(8,128)(2,1)}), bf16[2,1024,256]{1,2,0:T(8,128)(2,1)}) %all-reduce.16.cloned.1.call-update) | async-done | bytes 1048592 | tf_op jit(solution)/shard_map/psum | solution.py:57
  925.9 20.3 %collective-permute-done.5 = f32[2,256,256]{1,2,0:T(8,128)S(1)} collective-permute-done((f32[2,256,256]{1,2,0:T(8,128)S(1)}, f32[2,256,256]{1,2,0:T(8,128)S(1)}, u32[]{:S(2)}, u32[]{:S(2)}) %collective-permute-start.5) | collective-permute-done | bytes 524320 | tf_op jit(solution)/shard_map/ppermute | solution.py:14
  946.5 23.5 %custom-call.21 = f32[2,128,128]{2,1,0:T(8,128)S(1)} custom-call(f32[2,128,128]{2,1,0:T(8,128)S(1)} %cholesky.201), custom_call_target="Cholesky" | custom-call | tf_op jit(solution)/shard_map/jit(cholesky)/cholesky | solution.py:19
  990.4 23.5 %custom-call.23 = f32[2,128,128]{2,1,0:T(8,128)S(1)} custom-call(f32[2,128,128]{2,1,0:T(8,128)S(1)} %slice_subtract_fusion), custom_call_target="Cholesky" | custom-call | tf_op jit(solution)/shard_map/jit(cholesky)/cholesky | solution.py:19
  1018.4 39.5 %custom-call.24 = f32[2,2,128,128]{2,3,1,0:T(8,128)S(1)} custom-call(f32[2,2,128,128]{3,2,1,0:T(8,128)S(1)} %bitcast.142), custom_call_target="InvertDiagBlocksLowerTriangular" | custom-call | tf_op jit(solution)/shard_map/jit(_solve_triangular)/vmap()/triangular_solve | solution.py:20
  1067.4 72.9 %all-reduce.21 = bf16[512,2,256]{2,1,0:T(2,128)(2,1)} all-reduce(f32[512,2,256]{2,1,0:T(2,128)} %copy.99), channel_id=8, replica_groups=mesh['dp'=8,'mp'=4] {'dp'}, use_global_device_ids=true, to_apply=%region_12.15.clone | all-reduce | flops 262144 | bytes 1572864
  1141.2 31.7 %all_gather.27 = bf16[512,2,256]{2,1,0:T(2,128)(2,1)S(1)} all-gather(bf16[64,2,256]{2,1,0:T(2,128)(2,1)S(1)} %dynamic-slice_convert_fusion), channel_id=1, replica_groups=mesh['dp'=8,'mp'=4] {'dp'}, dimensions={0}, use_global_device_ids=true | all-gather | bytes 589824 | tf_op jit(solution)/shard_map/all_gather | solution.py:33
  1184.5 35.0 %reduce-scatter.8.cloned.1.call-done = bf16[2,3584,64]{1,2,0:T(8,128)(2,1)} async-done(((bf16[2,3584,256]{1,2,0:T(8,128)(2,1)}), bf16[2,3584,64]{1,2,0:T(8,128)(2,1)}) %reduce-scatter.8.cloned.1.call-update) | async-done | bytes 917520 | tf_op jit(solution)/shard_map/reduce_scatter | solution.py:62
  (135 shorter events, 265.5 us)
Async XLA Ops:
  7.2 1.2 copy-start
  7.2 173.0 %reduce-scatter.10.cloned.1.call-start = ((), (), s32[]{:S(2)}) async-start(), calls=%async_computation.8 | async-start | bytes 4587520
  10.7 75.1 %copy-start.7 = (u32[32]{0:T(128)S(1)}, u32[32]{0:T(128)}, u32[]{:S(2)}) copy-start(u32[32]{0:T(128)} %constant.98) | copy-start | bytes 388
  140.1 76.7 %all-gather.3.cloned.1.call-start = ((), (), s32[]{:S(2)}) async-start(), calls=%async_computation.3 | async-start | bytes 4587520 | tf_op jit(solution)/shard_map/all_gather | solution.py:45
  185.1 177.7 %all-reduce.14.cloned.1.call-start = ((), (), s32[]{:S(2)}) async-start(), calls=%async_computation.4 | async-start | bytes 2097152 | tf_op jit(solution)/shard_map/psum | solution.py:57
  329.3 382.1 %reduce-scatter.12.cloned.1.call-start = ((), (), s32[]{:S(2)}) async-start(), calls=%async_computation.9 | async-start | bytes 4587520
  364.9 28.3 %copy-start.1 = (bf16[2,1024,256]{1,2,0:T(8,128)(2,1)S(1)}, bf16[2,1024,256]{1,2,0:T(8,128)(2,1)}, u32[]{:S(2)}) copy-start(bf16[2,1024,256]{1,2,0:T(8,128)(2,1)} %all-reduce.14.cloned.1.call-done) | copy-start | bytes 3145732
  364.9 13.5 %collective-permute-start = (f32[2,256,256]{1,2,0:T(8,128)S(1)}, f32[2,256,256]{1,2,0:T(8,128)S(1)}, u32[]{:S(2)}, u32[]{:S(2)}) collective-permute-start(f32[2,256,256]{1,2,0:T(8,128)S(1)} %fusion.43), channel_id=1, source_target_pairs={{0,4},{4,0},{8,12},{12,8},{16,20},{20,16},{24,28},{28,24},{1,5},{5... | collective-permute-start | bytes 1572872 | tf_op jit(solution)/shard_map/ppermute | solution.py:14
  378.5 12.6 %collective-permute-start.1 = (f32[2,256,256]{1,2,0:T(8,128)S(1)}, f32[2,256,256]{1,2,0:T(8,128)S(1)}, u32[]{:S(2)}, u32[]{:S(2)}) collective-permute-start(f32[2,256,256]{1,2,0:T(8,128)S(1)} %add.68), channel_id=1, source_target_pairs={{0,8},{4,12},{8,0},{12,4},{16,24},{20,28},{24,16},{28,20},{1,9},{5... | collective-permute-start | bytes 1572872 | tf_op jit(solution)/shard_map/ppermute | solution.py:14
  391.1 23.8 %collective-permute-start.2 = (f32[2,256,256]{1,2,0:T(8,128)S(1)}, f32[2,256,256]{1,2,0:T(8,128)S(1)}, u32[]{:S(2)}, u32[]{:S(2)}) collective-permute-start(f32[2,256,256]{1,2,0:T(8,128)S(1)} %add.69), channel_id=1, source_target_pairs={{0,16},{4,20},{8,24},{12,28},{16,0},{20,4},{24,8},{28,12},{1,17},{... | collective-permute-start | bytes 1572872 | tf_op jit(solution)/shard_map/ppermute | solution.py:14
  415.3 0.8 copy-start.5
  460.1 80.3 %copy-start.3 = (f32[2,256,1024]{2,1,0:T(8,128)S(1)}, f32[2,256,1024]{2,1,0:T(8,128)}, u32[]{:S(2)}) copy-start(f32[2,256,1024]{2,1,0:T(8,128)} %convert_bitcast_fusion.1) | copy-start | bytes 6291460
  542.3 2.0 copy-start.6
  671.7 76.4 %all-gather.5.cloned.1.call-start = ((), (), s32[]{:S(2)}) async-start(), calls=%async_computation.5 | async-start | bytes 4587520 | tf_op jit(solution)/shard_map/all_gather | solution.py:45
  716.4 177.7 %all-reduce.16.cloned.1.call-start = ((), (), s32[]{:S(2)}) async-start(), calls=%async_computation.6 | async-start | bytes 2097152 | tf_op jit(solution)/shard_map/psum | solution.py:57
  860.6 358.9 %reduce-scatter.8.cloned.1.call-start = ((), (), s32[]{:S(2)}) async-start(), calls=%async_computation.7 | async-start | bytes 4587520 | tf_op jit(solution)/shard_map/reduce_scatter | solution.py:62
  896.1 28.2 %copy-start.2 = (bf16[2,1024,256]{1,2,0:T(8,128)(2,1)S(1)}, bf16[2,1024,256]{1,2,0:T(8,128)(2,1)}, u32[]{:S(2)}) copy-start(bf16[2,1024,256]{1,2,0:T(8,128)(2,1)} %all-reduce.16.cloned.1.call-done) | copy-start | bytes 3145732
  896.1 13.5 %collective-permute-start.3 = (f32[2,256,256]{1,2,0:T(8,128)S(1)}, f32[2,256,256]{1,2,0:T(8,128)S(1)}, u32[]{:S(2)}, u32[]{:S(2)}) collective-permute-start(f32[2,256,256]{1,2,0:T(8,128)S(1)} %fusion.44), channel_id=1, source_target_pairs={{0,4},{4,0},{8,12},{12,8},{16,20},{20,16},{24,28},{28,24},{1,5},{5... | collective-permute-start | bytes 1572872 | tf_op jit(solution)/shard_map/ppermute | solution.py:14
  909.7 12.6 %collective-permute-start.4 = (f32[2,256,256]{1,2,0:T(8,128)S(1)}, f32[2,256,256]{1,2,0:T(8,128)S(1)}, u32[]{:S(2)}, u32[]{:S(2)}) collective-permute-start(f32[2,256,256]{1,2,0:T(8,128)S(1)} %add.71), channel_id=1, source_target_pairs={{0,8},{4,12},{8,0},{12,4},{16,24},{20,28},{24,16},{28,20},{1,9},{5... | collective-permute-start | bytes 1572872 | tf_op jit(solution)/shard_map/ppermute | solution.py:14
  922.3 23.8 %collective-permute-start.5 = (f32[2,256,256]{1,2,0:T(8,128)S(1)}, f32[2,256,256]{1,2,0:T(8,128)S(1)}, u32[]{:S(2)}, u32[]{:S(2)}) collective-permute-start(f32[2,256,256]{1,2,0:T(8,128)S(1)} %add.72), channel_id=1, source_target_pairs={{0,16},{4,20},{8,24},{12,28},{16,0},{20,4},{24,8},{28,12},{1,17},{... | collective-permute-start | bytes 1572872 | tf_op jit(solution)/shard_map/ppermute | solution.py:14
  1181.5 38.0 %copy-start.4 = (f32[2,3584,64]{1,2,0:T(8,128)S(1)}, f32[2,3584,64]{1,2,0:T(8,128)}, u32[]{:S(2)}) copy-start(f32[2,3584,64]{1,2,0:T(8,128)} %param.12) | copy-start | bytes 5505028
Sparse Core Ops, SparseCore 0:
  140.2 39.8 reduce-scatter.9
  185.3 31.4 all-gather.2
  329.4 33.3 all-reduce.13
  671.8 39.5 reduce-scatter.11
  716.5 31.4 all-gather.4
  860.7 33.2 all-reduce.15
  1180.1 39.3 reduce-scatter.7
